TPU v7x, 512 devices: a whole 4x4x16 slice. The times are simulated.
512 devices in a mesh: seq: 64 (over y, z), req: 8 (over x, core).
Axes of the slice: x: 4, y: 4, z: 16, core: 2. Of those that a mesh axis runs over, the one named last changes fastest.
Arguments:
- new_token_queries: bfloat16 [4, 64, 2048], P(None, 'req'), may hold values from -48 to 48
- new_token_keys: bfloat16 [4, 64, 1024], P(None, 'req'), may hold values from -48 to 48
- new_token_values: bfloat16 [4, 64, 1024], P(None, 'req'), may hold values from -6 to 6
- key_cache: bfloat16 [64, 2048, 1024], P('req', 'seq'), may hold values from -48 to 48
- value_cache: bfloat16 [64, 2048, 1024], P('req', 'seq'), may hold values from -6 to 6
- cache_len: int32 [64], P('req'), may hold values from 1 to 2048, 34816 in all
- resid: bfloat16 [4, 64, 2048], P(None, 'req'), may hold values from -6 to 6
- gain: bfloat16 [2048], replicated, may hold values from 0.5 to 1.5
- w_gate: bfloat16 [2048, 6144], P('seq', 'req'), may hold values from -0.125 to 0.125
- w_up: bfloat16 [2048, 6144], P('seq', 'req'), may hold values from -0.125 to 0.125
- w_down: bfloat16 [6144, 2048], P('req', 'seq'), may hold values from -0.078125 to 0.078125
Outputs:
- out: bfloat16 [4, 64, 2048], P(None, 'req')
All inputs are finite; a program needn't handle non-finite values. No bound on the sum of `cache_len` on one device may be relied on, other than what follows from the above.
Results may differ from a plain program's by a relative error of at most 0.006.
Values may be sent and summed in bfloat16 or wider, within the bound.
A program may use at most 128 MiB of HBM per device.

v0:
```python
import math
import jax
import jax.numpy as jnp
from jax import lax
from jax.sharding import PartitionSpec as P

QUERY_HEADS = 16
KEY_VALUE_HEADS = 8
HEAD_SIZE = 128
DECODE_STEPS = 4
NEG_FILL = -1e30
EPSILON = 1e-06


def page_partial(query_vector, key_row_set, value_row_set, valid):
    scores = jnp.einsum(
        "rkgd,rbkd->rkgb", query_vector, key_row_set, preferred_element_type=jnp.float32
    ) / math.sqrt(HEAD_SIZE)
    inside = valid[:, None, None, :]
    scores = jnp.where(inside, scores, NEG_FILL)
    highest = jnp.max(scores, axis=-1)
    weights = jnp.where(inside, jnp.exp(scores - highest[..., None]), 0.0).astype(jnp.bfloat16)
    totals = jnp.sum(weights.astype(jnp.float32), axis=-1)
    weighted = jnp.einsum(
        "rkgb,rbkd->rkgd", weights, value_row_set, preferred_element_type=jnp.float32
    )
    return (highest, totals, weighted)


def merge_pair(former, latter):
    highest = jnp.maximum(former[0], latter[0])
    first_scale = jnp.exp(former[0] - highest)
    second_scale = jnp.exp(latter[0] - highest)
    totals = first_scale * former[1] + second_scale * latter[1]
    weighted = first_scale[..., None] * former[2] + second_scale[..., None] * latter[2]
    return (highest, totals, weighted)


def body(
    new_token_queries,
    new_token_keys,
    new_token_values,
    key_cache,
    value_cache,
    cache_len,
    resid,
    gain,
    w_gate,
    w_up,
    w_down,
):
    count_of_rows = new_token_queries.shape[1]
    page_length = key_cache.shape[1]
    head_cluster = QUERY_HEADS // KEY_VALUE_HEADS
    slice_width = w_gate.shape[0]
    unit_count = w_gate.shape[1]
    seq_index = lax.axis_index("seq")
    positions = seq_index * page_length + jnp.arange(page_length, dtype=jnp.int32)
    valid = positions[None, :] < cache_len[:, None]
    key_row_set = key_cache.reshape(count_of_rows, page_length, KEY_VALUE_HEADS, HEAD_SIZE)
    value_row_set = value_cache.reshape(count_of_rows, page_length, KEY_VALUE_HEADS, HEAD_SIZE)
    joined = jnp.concatenate([w_gate, w_up], axis=1)
    gain_scale = gain.astype(jnp.float32)
    results = []
    for decode_step_index in range(DECODE_STEPS):
        query_vector = new_token_queries[decode_step_index].reshape(
            count_of_rows, KEY_VALUE_HEADS, head_cluster, HEAD_SIZE
        )
        local = page_partial(query_vector, key_row_set, value_row_set, valid)
        highest = lax.pmax(local[0], "seq")
        factor = jnp.exp(local[0] - highest)
        totals, weighted = lax.psum((factor * local[1], factor[..., None] * local[2]), "seq")
        incoming_keys = jnp.swapaxes(new_token_keys[: decode_step_index + 1], 0, 1).reshape(
            count_of_rows, decode_step_index + 1, KEY_VALUE_HEADS, HEAD_SIZE
        )
        incoming_values = jnp.swapaxes(new_token_values[: decode_step_index + 1], 0, 1).reshape(
            count_of_rows, decode_step_index + 1, KEY_VALUE_HEADS, HEAD_SIZE
        )
        fresh_valid = jnp.ones((count_of_rows, decode_step_index + 1), jnp.bool_)
        fresh = page_partial(query_vector, incoming_keys, incoming_values, fresh_valid)
        combined = merge_pair((highest, totals, weighted), fresh)
        attention = (
            (combined[2] / combined[1][..., None])
            .reshape(count_of_rows, QUERY_HEADS * HEAD_SIZE)
            .astype(jnp.bfloat16)
        )
        attention = lax.optimization_barrier(attention).astype(jnp.float32)
        stream = (resid[decode_step_index].astype(jnp.float32) + attention).astype(jnp.bfloat16)
        stream = lax.optimization_barrier(stream).astype(jnp.float32)
        scaled = lax.rsqrt(jnp.mean(stream * stream, axis=-1, keepdims=True) + EPSILON)
        normed = (stream * scaled * gain_scale).astype(jnp.bfloat16)
        own_slice = lax.dynamic_slice_in_dim(normed, seq_index * slice_width, slice_width, 1)
        partial_sums = jnp.dot(
            lax.all_gather(own_slice, "req", axis=0, tiled=True),
            joined,
            preferred_element_type=jnp.float32,
        )
        whole_sums = lax.psum(partial_sums, "seq")
        hidden = (jax.nn.silu(whole_sums[:, :unit_count]) * whole_sums[:, unit_count:]).astype(
            jnp.bfloat16
        )
        down_sum = lax.psum_scatter(
            jnp.dot(hidden, w_down, preferred_element_type=jnp.float32),
            "req",
            scatter_dimension=0,
            tiled=True,
        )
        stream_slice = lax.dynamic_slice_in_dim(stream, seq_index * slice_width, slice_width, 1)
        out_piece = (stream_slice + down_sum).astype(jnp.bfloat16)
        results.append(lax.all_gather(out_piece, "seq", axis=1, tiled=True))
    return jnp.stack(results)


def solution(mesh):
    placed = (
        P(None, "req", None),
        P(None, "req", None),
        P(None, "req", None),
        P("req", "seq", None),
        P("req", "seq", None),
        P("req"),
        P(None, "req", None),
        P(),
        P("seq", "req"),
        P("seq", "req"),
        P("req", "seq"),
    )
    return jax.shard_map(
        body, mesh=mesh, in_specs=placed, out_specs=P(None, "req", None), check_vma=False
    )
```

profile of v0, /device:TPU:8, one launch (start us, length us, event | category | flops | bytes accessed | tf_op | source)
XLA Modules:
  0.0 1327.7 jit_solution(7573360003918362906)
XLA Ops:
  6.5 0.9 fusion.88
  7.5 0.6 copy-done.7
  8.2 1.5 fusion.89
  9.7 0.5 fusion.90
  10.2 0.5 fusion.91
  10.7 0.5 fusion.92
  11.1 261.7 %all-reduce.7 = (f32[8,8,2]{2,1,0:T(8,128)S(1)}, f32[8,8,2]{2,1,0:T(8,128)S(1)}, f32[8,8,2]{2,1,0:T(8,128)S(1)}, f32[8,8,2]{2,1,0:T(8,128)S(1)}) all-reduce(f32[8,8,2]{2,1,0:T(8,128)S(1)} %get-tuple-element.80, f32[8,8,2]{2,1,0:T(8,128)S(1)} %get-tuple-element.78, ...), channel_id=1, replica_groups=mesh['seq'=64,'req'=8] {'seq'}, use_global_device_ids=true, to_apply=%region_29.30 | all-reduce | flops 512 | bytes 4096 | tf_op jit(solution)/shard_map/pmax | solution.py:70
  272.8 0.7 convert_reduce_fusion.5
  273.5 0.9 convolution_multiply_fusion.11
  274.4 0.9 convolution_multiply_fusion.9
  275.3 0.9 convolution_multiply_fusion.7
  276.2 0.9 convolution_multiply_fusion.5
  277.1 0.8 copy-done.1
  278.0 0.3 fusion.94
  278.3 0.3 fusion.93
  278.6 0.2 fusion.59
  278.8 0.2 copy.118
  279.0 0.2 fusion.61
  279.2 0.6 copy-done.5
  279.8 0.3 convert_reduce_fusion.2
  280.1 274.1 %all-reduce.4 = (f32[8,8,2]{2,1,0:T(8,128)S(1)}, f32[8,8,2]{2,1,0:T(8,128)S(1)}, f32[8,8,2]{2,1,0:T(8,128)S(1)}, f32[8,8,2]{2,1,0:T(8,128)S(1)}) all-reduce(f32[8,8,2]{2,1,0:T(8,128)S(1)} %get-tuple-element.88, f32[8,8,2]{2,1,0:T(8,128)S(1)} %get-tuple-element.47, ...), channel_id=1, replica_groups=mesh['seq'=64,'req'=8] {'seq'}, use_global_device_ids=true, to_apply=%region_33.34 | all-reduce | flops 512 | bytes 4096 | tf_op jit(solution)/shard_map/psum | solution.py:72
  554.2 0.3 convert_reduce_fusion
  554.5 0.8 copy-done.6
  555.4 0.1 copy.124
  555.5 0.2 copy.122
  555.7 0.8 dynamic-slice.8
  556.6 1.2 fusion.11
  557.8 0.8 copy-done.13
  558.6 0.4 fusion.12
  559.0 0.8 copy-done.12
  559.8 0.3 fusion.10
  560.1 0.8 copy-done.4
  561.0 0.3 fusion.45
  561.3 0.5 copy-done.3
  561.9 0.1 multiply_reduce_fusion
  562.0 0.1 multiply_reduce_fusion.1
  562.2 0.1 multiply_reduce_fusion.2
  562.3 0.1 multiply_reduce_fusion.3
  562.6 12.0 all_gather.24
  574.6 11.2 all_gather.26
  585.8 0.9 fusion.95
  586.8 0.9 fusion.96
  587.7 11.3 all_gather.28
  599.0 0.9 fusion.97
  599.9 11.2 all_gather.30
  611.2 0.9 fusion.98
  612.1 1.3 dynamic-slice
  614.0 286.2 %all-reduce.12.cloned.1.call-done = (f32[64,1536]{1,0:T(8,128)}, f32[64,1536]{1,0:T(8,128)}, f32[64,1536]{1,0:T(8,128)}, f32[64,1536]{1,0:T(8,128)}) async-done(((f32[64,1536]{1,0:T(8,128)}, f32[64,1536]{1,0:T(8,128)}, f32[64,1536]{1,0:T(8,128)}, f32[64,1536]{1,0:T(8,128)}), (f32[64,1536]{1,0:T(8,128)}, f32[64,1536]{1,0:T(8,128)}, f32[64,1536]{1,0:T(8,128)}, ...) | async-done | bytes 1572880 | tf_op jit(solution)/shard_map/psum | solution.py:98
  900.2 1.2 fusion.33
  901.5 0.2 fusion.35
  901.7 0.8 copy-done.10
  902.5 0.2 fusion.37
  902.7 0.8 copy-done.9
  903.5 0.2 fusion.39
  903.7 24.8 %all-reduce.8 = (f32[64,32]{1,0:T(8,128)S(1)}, f32[64,32]{1,0:T(8,128)S(1)}, f32[64,32]{1,0:T(8,128)S(1)}, f32[64,32]{1,0:T(8,128)S(1)}) all-reduce(f32[64,32]{1,0:T(8,128)S(1)} %fusion.39, f32[64,32]{1,0:T(8,128)S(1)} %fusion.37, f32[64,32]{1,0:T(8,128)S(1)} %fusion.35, ...), channel_id=5, replica_groups=mesh['seq'=64,'req'=8] {'req'}, use_global_device_ids=true, to_apply=%region_37.38.clone | all-reduce | flops 8192 | bytes 65536
  928.6 97.9 %all-gather = bf16[64,32,8]{1,2,0:T(8,128)(2,1)S(1)} all-gather(bf16[1,32,8]{1,2,0:T(8,128)(2,1)S(1)} %fusion.68), channel_id=1, replica_groups=mesh['seq'=64,'req'=8] {'seq'}, dimensions={0}, use_global_device_ids=true | all-gather | bytes 33280 | tf_op jit(solution)/shard_map/all_gather | solution.py:110
  1026.5 0.2 reshape.168
  1026.8 97.5 %all-gather.1 = bf16[64,32,8]{1,2,0:T(8,128)(2,1)S(1)} all-gather(bf16[1,32,8]{1,2,0:T(8,128)(2,1)S(1)} %fusion.69), channel_id=1, replica_groups=mesh['seq'=64,'req'=8] {'seq'}, dimensions={0}, use_global_device_ids=true | all-gather | bytes 33280 | tf_op jit(solution)/shard_map/all_gather | solution.py:110
  1124.3 0.2 reshape.170
  1124.5 97.6 %all-gather.2 = bf16[64,32,8]{1,2,0:T(8,128)(2,1)S(1)} all-gather(bf16[1,32,8]{1,2,0:T(8,128)(2,1)S(1)} %fusion.70), channel_id=1, replica_groups=mesh['seq'=64,'req'=8] {'seq'}, dimensions={0}, use_global_device_ids=true | all-gather | bytes 33280 | tf_op jit(solution)/shard_map/all_gather | solution.py:110
  1222.2 0.2 reshape.172
  1222.5 97.5 %all-gather.3 = bf16[64,32,8]{1,2,0:T(8,128)(2,1)S(1)} all-gather(bf16[1,32,8]{1,2,0:T(8,128)(2,1)S(1)} %fusion.71), channel_id=1, replica_groups=mesh['seq'=64,'req'=8] {'seq'}, dimensions={0}, use_global_device_ids=true | all-gather | bytes 33280 | tf_op jit(solution)/shard_map/all_gather | solution.py:110
  1320.0 0.2 reshape.174
  1320.2 0.7 pad_maximum_fusion
  (75 shorter events, 1.3 us)
Async XLA Ops:
  6.5 267.0 %copy-start = (bf16[8,32,1024]{2,1,0:T(8,128)(2,1)S(1)}, bf16[8,32,1024]{2,1,0:T(8,128)(2,1)}, u32[]{:S(2)}) copy-start(bf16[8,32,1024]{2,1,0:T(8,128)(2,1)} %param.15) | copy-start | bytes 1572868
  6.5 550.0 %all-reduce.14.cloned.1.call-start = ((), (), s32[]{:S(2)}) async-start(), calls=%async_computation.1 | async-start | bytes 524288 | tf_op jit(solution)/shard_map/psum | solution.py:72
  7.4 0.7 copy-start.7
  7.5 2.2 copy-start.8
  277.0 0.8 copy-start.1
  277.1 0.9 copy-start.2
  277.1 623.2 %all-reduce.12.cloned.1.call-start = ((), (), s32[]{:S(2)}) async-start(), calls=%async_computation | async-start | bytes 3145728 | tf_op jit(solution)/shard_map/psum | solution.py:98
  279.0 0.8 copy-start.5
  554.5 0.8 copy-start.6
  557.8 0.8 copy-start.13
  559.0 0.8 copy-start.12
  560.1 0.8 copy-start.4
  561.0 0.9 copy-start.3
  612.1 288.2 %copy-start.14 = (bf16[768,32]{0,1:T(8,128)(2,1)S(1)}, bf16[768,32]{0,1:T(8,128)(2,1)}, u32[]{:S(2)}) copy-start(bf16[768,32]{0,1:T(8,128)(2,1)} %param.21) | copy-start | bytes 147460
  900.2 1.3 copy-start.11
  901.5 1.0 copy-start.10
  902.5 1.0 copy-start.9
Sparse Core Ops, SparseCore 0:
  277.2 274.5 all-reduce.13
  612.2 287.9 all-reduce.11
where the time goes:
time: 1330 us
  blocking collectives  997 us (75%)
  waiting for transfers between devices  286 us (22%)
  matrix products  14.7 us (1%)
  between operations  14.5 us (1%)
    all_gather x4, blocking collectives, body(): results.append(lax.all_gather(out_piece, 'seq', axis=1, tiled=True))  391 us
    psum x1, waiting for transfers between devices, body(): whole_sums = lax.psum(partial_sums, 'seq')  286 us
    psum x1, blocking collectives, body(): lax.psum((factor * local[1], factor[..., None] * local[2]), 'seq')  274 us
    pmax x1, blocking collectives, body(): highest = lax.pmax(local[0], 'seq')  262 us
    all_gather x4, blocking collectives, body(): lax.all_gather(own_slice, 'req', axis=0, tiled=True)  45.8 us
  transfers between devices with their start and end apart: 2, of which 1 were waited for; matrix products, arithmetic and copies ran while one was open for 0% of the time, Pallas kernels for 0%

commit v1 on v0

--- a/solution.py
+++ b/solution.py
@@ -10,6 +10,13 @@
 DECODE_STEPS = 4
 NEG_FILL = -1e30
 EPSILON = 1e-06
+
+
+def all_by_exchange(x, mesh_axis, d):
+    n_dev = lax.axis_size(mesh_axis)
+    shards = jnp.stack([x for _ in range(n_dev)])
+    shards = lax.all_to_all(shards, mesh_axis, split_axis=0, concat_axis=0)
+    return jnp.concatenate(shards, axis=d)
 
 
 def page_partial(query_vector, key_row_set, value_row_set, valid):
@@ -107,7 +114,7 @@
         )
         stream_slice = lax.dynamic_slice_in_dim(stream, seq_index * slice_width, slice_width, 1)
         out_piece = (stream_slice + down_sum).astype(jnp.bfloat16)
-        results.append(lax.all_gather(out_piece, "seq", axis=1, tiled=True))
+        results.append(all_by_exchange(out_piece, "seq", 1))
     return jnp.stack(results)
 
 

time: 1330 us -> 1020 us (0.77)
  blocking collectives: 997 us -> 606 us
  waiting for transfers between devices: 286 us -> 337 us
  starting transfers between devices: 0.04 us -> 26.9 us
    all_gather x4 -> x0, blocking collectives: 391 us -> none  [body(): results.append(lax.all_gather(out_piece, 'seq', axis=1, tiled=True))]
    all_to_all x0 -> x4, waiting for transfers between devices: none -> 50.4 us  [all_by_exchange(): shards = lax.all_to_all(shards, mesh_axis, split_axis=0, concat_axis=0)]
    all_to_all x0 -> x4, starting transfers between devices: none -> 26.9 us  [all_by_exchange(): shards = lax.all_to_all(shards, mesh_axis, split_axis=0, concat_axis=0)]
  transfers between devices with their start and end apart: 2 -> 6, of which waited for: 1 -> 5; matrix products, arithmetic and copies ran while one was open for 0% -> 1% of each run, Pallas kernels for 0% -> 0%
where the time goes in v1:
time: 1020 us
  blocking collectives  606 us (59%)
  waiting for transfers between devices  337 us (33%)
  starting transfers between devices  26.9 us (3%)
  local copies, waits for them, and re-layouts  15.3 us (2%)
  matrix products  14.7 us (1%)
  between operations  14.6 us (1%)
    psum x1, waiting for transfers between devices, body(): whole_sums = lax.psum(partial_sums, 'seq')  286 us
    psum x1, blocking collectives, body(): lax.psum((factor * local[1], factor[..., None] * local[2]), 'seq')  274 us
    pmax x1, blocking collectives, body(): highest = lax.pmax(local[0], 'seq')  262 us
    all_to_all x4, waiting for transfers between devices, all_by_exchange(): shards = lax.all_to_all(shards, mesh_axis, split_axis=0, concat_axis=0)  50.4 us
    all_gather x4, blocking collectives, body(): lax.all_gather(own_slice, 'req', axis=0, tiled=True)  45.6 us
    all_to_all x4, starting transfers between devices, all_by_exchange(): shards = lax.all_to_all(shards, mesh_axis, split_axis=0, concat_axis=0)  26.9 us
    unnamed x1, blocking collectives  24.8 us
  transfers between devices with their start and end apart: 6, of which 5 were waited for; matrix products, arithmetic and copies ran while one was open for 1% of the time, Pallas kernels for 0%

profile of v1, /device:TPU:8, one launch (start us, length us, event | category | flops | bytes accessed | tf_op | source)
XLA Modules:
  0.0 1018.1 jit_solution(733708506438381974)
XLA Ops:
  6.5 0.9 fusion.84
  7.5 0.6 copy-done.7
  8.2 1.5 fusion.85
  9.7 0.5 fusion.86
  10.2 0.5 fusion.87
  10.7 0.5 fusion.88
  11.1 261.7 %all-reduce.7 = (f32[8,8,2]{2,1,0:T(8,128)S(1)}, f32[8,8,2]{2,1,0:T(8,128)S(1)}, f32[8,8,2]{2,1,0:T(8,128)S(1)}, f32[8,8,2]{2,1,0:T(8,128)S(1)}) all-reduce(f32[8,8,2]{2,1,0:T(8,128)S(1)} %get-tuple-element.80, f32[8,8,2]{2,1,0:T(8,128)S(1)} %get-tuple-element.78, ...), channel_id=1, replica_groups=mesh['seq'=64,'req'=8] {'seq'}, use_global_device_ids=true, to_apply=%region_29.30 | all-reduce | flops 512 | bytes 4096 | tf_op jit(solution)/shard_map/pmax | solution.py:77
  272.8 0.7 convert_reduce_fusion.5
  273.5 0.9 convolution_multiply_fusion.11
  274.4 0.9 convolution_multiply_fusion.9
  275.3 0.9 convolution_multiply_fusion.7
  276.2 0.9 convolution_multiply_fusion.5
  277.1 0.8 copy-done.1
  278.0 0.3 fusion.90
  278.3 0.3 fusion.89
  278.6 0.2 fusion.59
  278.8 0.2 copy.114
  279.0 0.2 fusion.61
  279.2 0.6 copy-done.5
  279.8 0.3 convert_reduce_fusion.2
  280.1 274.2 %all-reduce.4 = (f32[8,8,2]{2,1,0:T(8,128)S(1)}, f32[8,8,2]{2,1,0:T(8,128)S(1)}, f32[8,8,2]{2,1,0:T(8,128)S(1)}, f32[8,8,2]{2,1,0:T(8,128)S(1)}) all-reduce(f32[8,8,2]{2,1,0:T(8,128)S(1)} %get-tuple-element.88, f32[8,8,2]{2,1,0:T(8,128)S(1)} %get-tuple-element.47, ...), channel_id=1, replica_groups=mesh['seq'=64,'req'=8] {'seq'}, use_global_device_ids=true, to_apply=%region_33.34 | all-reduce | flops 512 | bytes 4096 | tf_op jit(solution)/shard_map/psum | solution.py:79
  554.2 0.3 convert_reduce_fusion
  554.6 0.8 copy-done.6
  555.6 0.2 copy.118
  555.8 0.8 dynamic-slice.8
  556.6 1.2 fusion.11
  557.9 0.8 copy-done.13
  558.7 0.4 fusion.12
  559.1 0.8 copy-done.12
  559.9 0.3 fusion.10
  560.2 0.8 copy-done.4
  561.0 0.3 fusion.45
  561.4 0.5 copy-done.3
  562.7 11.9 %all_gather.12 = bf16[64,32]{1,0:T(8,128)(2,1)S(1)} all-gather(bf16[8,32]{1,0:T(8,128)(2,1)S(1)} %get-tuple-element.70), channel_id=1, replica_groups=mesh['seq'=64,'req'=8] {'req'}, dimensions={0}, use_global_device_ids=true | all-gather | bytes 4608 | tf_op jit(solution)/shard_map/all_gather | solution.py:101
  574.5 11.2 %all_gather.13 = bf16[64,32]{1,0:T(8,128)(2,1)S(1)} all-gather(bf16[8,32]{1,0:T(8,128)(2,1)S(1)} %get-tuple-element.71), channel_id=1, replica_groups=mesh['seq'=64,'req'=8] {'req'}, dimensions={0}, use_global_device_ids=true | all-gather | bytes 4608 | tf_op jit(solution)/shard_map/all_gather | solution.py:101
  585.7 0.9 fusion.91
  586.7 0.9 fusion.92
  587.6 11.3 %all_gather.14 = bf16[64,32]{1,0:T(8,128)(2,1)S(1)} all-gather(bf16[8,32]{1,0:T(8,128)(2,1)S(1)} %get-tuple-element.72), channel_id=1, replica_groups=mesh['seq'=64,'req'=8] {'req'}, dimensions={0}, use_global_device_ids=true | all-gather | bytes 4608 | tf_op jit(solution)/shard_map/all_gather | solution.py:101
  598.9 1.0 fusion.93
  599.9 11.2 %all_gather.15 = bf16[64,32]{1,0:T(8,128)(2,1)S(1)} all-gather(bf16[8,32]{1,0:T(8,128)(2,1)S(1)} %get-tuple-element.73), channel_id=1, replica_groups=mesh['seq'=64,'req'=8] {'req'}, dimensions={0}, use_global_device_ids=true | all-gather | bytes 4608 | tf_op jit(solution)/shard_map/all_gather | solution.py:101
  611.1 0.9 fusion.94
  612.0 1.3 dynamic-slice
  614.0 286.4 %all-reduce.12.cloned.1.call-done = (f32[64,1536]{1,0:T(8,128)}, f32[64,1536]{1,0:T(8,128)}, f32[64,1536]{1,0:T(8,128)}, f32[64,1536]{1,0:T(8,128)}) async-done(((f32[64,1536]{1,0:T(8,128)}, f32[64,1536]{1,0:T(8,128)}, f32[64,1536]{1,0:T(8,128)}, f32[64,1536]{1,0:T(8,128)}), (f32[64,1536]{1,0:T(8,128)}, f32[64,1536]{1,0:T(8,128)}, f32[64,1536]{1,0:T(8,128)}, ...) | async-done | bytes 1572880 | tf_op jit(solution)/shard_map/psum | solution.py:105
  900.3 1.2 fusion.33
  901.6 0.2 fusion.35
  901.8 0.8 copy-done.10
  902.6 0.2 fusion.37
  902.8 0.8 copy-done.9
  903.6 0.2 fusion.39
  903.8 24.8 %all-reduce.8 = (f32[64,32]{1,0:T(8,128)S(1)}, f32[64,32]{1,0:T(8,128)S(1)}, f32[64,32]{1,0:T(8,128)S(1)}, f32[64,32]{1,0:T(8,128)S(1)}) all-reduce(f32[64,32]{1,0:T(8,128)S(1)} %fusion.39, f32[64,32]{1,0:T(8,128)S(1)} %fusion.37, f32[64,32]{1,0:T(8,128)S(1)} %fusion.35, ...), channel_id=5, replica_groups=mesh['seq'=64,'req'=8] {'req'}, use_global_device_ids=true, to_apply=%region_37.38.clone | all-reduce | flops 8192 | bytes 65536
  928.7 0.7 reshape.203
  929.4 10.5 %all-to-all-start = ((bf16[64,2,128]{2,1,0:T(2,128)(2,1)}), bf16[64,2,128]{2,1,0:T(2,128)(2,1)S(1)}, u32[]{:S(2)}, u32[]{:S(2)}) async-start(bf16[64,2,128]{2,1,0:T(2,128)(2,1)} %reshape.203), calls=%async_computation | async-start | bytes 65536 | tf_op jit(solution)/shard_map/all_to_all | solution.py:18
  940.0 0.7 reshape.201
  940.7 12.6 %all-to-all-done = bf16[64,2,128]{2,1,0:T(2,128)(2,1)S(1)} async-done(((bf16[64,2,128]{2,1,0:T(2,128)(2,1)}), bf16[64,2,128]{2,1,0:T(2,128)(2,1)S(1)}, u32[]{:S(2)}, u32[]{:S(2)}) %all-to-all-start) | async-done | bytes 32800 | tf_op jit(solution)/shard_map/all_to_all | solution.py:18
  953.4 5.5 all-to-all-start.1
  959.0 0.7 reshape.199
  959.8 12.6 %all-to-all-done.1 = bf16[64,2,128]{2,1,0:T(2,128)(2,1)S(1)} async-done(((bf16[64,2,128]{2,1,0:T(2,128)(2,1)}), bf16[64,2,128]{2,1,0:T(2,128)(2,1)S(1)}, u32[]{:S(2)}, u32[]{:S(2)}) %all-to-all-start.1) | async-done | bytes 32800 | tf_op jit(solution)/shard_map/all_to_all | solution.py:18
  972.4 5.5 all-to-all-start.2
  978.0 0.7 reshape.197
  978.8 12.7 %all-to-all-done.2 = bf16[64,2,128]{2,1,0:T(2,128)(2,1)S(1)} async-done(((bf16[64,2,128]{2,1,0:T(2,128)(2,1)}), bf16[64,2,128]{2,1,0:T(2,128)(2,1)S(1)}, u32[]{:S(2)}, u32[]{:S(2)}) %all-to-all-start.2) | async-done | bytes 32800 | tf_op jit(solution)/shard_map/all_to_all | solution.py:18
  991.4 5.4 all-to-all-start.3
  996.9 0.2 stack_reshape.12
  997.7 12.5 %all-to-all-done.3 = bf16[64,2,128]{2,1,0:T(2,128)(2,1)S(1)} async-done(((bf16[64,2,128]{2,1,0:T(2,128)(2,1)}), bf16[64,2,128]{2,1,0:T(2,128)(2,1)S(1)}, u32[]{:S(2)}, u32[]{:S(2)}) %all-to-all-start.3) | async-done | bytes 32800 | tf_op jit(solution)/shard_map/all_to_all | solution.py:18
  1010.6 0.7 pad_maximum_fusion
  (91 shorter events, 3.0 us)
Async XLA Ops:
  6.5 267.0 %copy-start = (bf16[8,32,1024]{2,1,0:T(8,128)(2,1)S(1)}, bf16[8,32,1024]{2,1,0:T(8,128)(2,1)}, u32[]{:S(2)}) copy-start(bf16[8,32,1024]{2,1,0:T(8,128)(2,1)} %param.15) | copy-start | bytes 1572868
  6.5 550.1 %all-reduce.14.cloned.1.call-start = ((), (), s32[]{:S(2)}) async-start(), calls=%async_computation.5 | async-start | bytes 524288 | tf_op jit(solution)/shard_map/psum | solution.py:79
  7.4 0.7 copy-start.7
  7.5 2.2 copy-start.8
  277.0 0.8 copy-start.1
  277.1 0.9 copy-start.2
  277.1 623.2 %all-reduce.12.cloned.1.call-start = ((), (), s32[]{:S(2)}) async-start(), calls=%async_computation.4 | async-start | bytes 3145728 | tf_op jit(solution)/shard_map/psum | solution.py:105
  279.0 0.8 copy-start.5
  554.6 0.8 copy-start.6
  557.8 0.8 copy-start.13
  559.1 0.8 copy-start.12
  560.2 0.8 copy-start.4
  561.0 0.9 copy-start.3
  612.0 288.3 %copy-start.14 = (bf16[768,32]{0,1:T(8,128)(2,1)S(1)}, bf16[768,32]{0,1:T(8,128)(2,1)}, u32[]{:S(2)}) copy-start(bf16[768,32]{0,1:T(8,128)(2,1)} %param.21) | copy-start | bytes 147460
  900.3 1.3 copy-start.11
  901.6 1.0 copy-start.10
  902.6 1.0 copy-start.9
  929.4 24.0 %all-to-all-start = ((bf16[64,2,128]{2,1,0:T(2,128)(2,1)}), bf16[64,2,128]{2,1,0:T(2,128)(2,1)S(1)}, u32[]{:S(2)}, u32[]{:S(2)}) async-start(bf16[64,2,128]{2,1,0:T(2,128)(2,1)} %reshape.203), calls=%async_computation | async-start | bytes 65536 | tf_op jit(solution)/shard_map/all_to_all | solution.py:18
  953.4 19.0 %all-to-all-start.1 = ((bf16[64,2,128]{2,1,0:T(2,128)(2,1)}), bf16[64,2,128]{2,1,0:T(2,128)(2,1)S(1)}, u32[]{:S(2)}, u32[]{:S(2)}) async-start(bf16[64,2,128]{2,1,0:T(2,128)(2,1)} %reshape.201), calls=%async_computation.1 | async-start | bytes 65536 | tf_op jit(solution)/shard_map/all_to_all | solution.py:18
  972.4 19.0 %all-to-all-start.2 = ((bf16[64,2,128]{2,1,0:T(2,128)(2,1)}), bf16[64,2,128]{2,1,0:T(2,128)(2,1)S(1)}, u32[]{:S(2)}, u32[]{:S(2)}) async-start(bf16[64,2,128]{2,1,0:T(2,128)(2,1)} %reshape.199), calls=%async_computation.2 | async-start | bytes 65536 | tf_op jit(solution)/shard_map/all_to_all | solution.py:18
  991.4 18.8 %all-to-all-start.3 = ((bf16[64,2,128]{2,1,0:T(2,128)(2,1)}), bf16[64,2,128]{2,1,0:T(2,128)(2,1)S(1)}, u32[]{:S(2)}, u32[]{:S(2)}) async-start(bf16[64,2,128]{2,1,0:T(2,128)(2,1)} %reshape.197), calls=%async_computation.3 | async-start | bytes 65536 | tf_op jit(solution)/shard_map/all_to_all | solution.py:18
Sparse Core Ops, SparseCore 0:
  277.2 274.5 all-reduce.13
  612.2 288.1 all-reduce.11
